TPU v7x, 128 devices: a whole 4x4x4 slice. The times are simulated.
128 devices in a mesh: ctx: 64 (over x_lo, y, z, core), head: 2 (over x_hi).
Axes of the slice: x: 4 (x_hi: 2, x_lo: 2; x = x_hi * 2 + x_lo), y: 4, z: 4, core: 2. Of those that a mesh axis runs over, the one named last changes fastest.
Arguments:
- queries: bfloat16 [32768, 1024], P(('ctx', 'head')), may hold values from -9 to 9
- keys_in: bfloat16 [32768, 1024], P(('ctx', 'head')), may hold values from -9 to 9
- values: bfloat16 [32768, 1024], P(('ctx', 'head')), may hold values from -6 to 6
- d_out: bfloat16 [32768, 1024], P(('ctx', 'head')), may hold values from -6 to 6
- pair_blocks: int32 [512, 16], replicated, may hold values from 0 to 511, as said below
- pair_count: int32 [512], replicated, may hold values from 1 to 16, as said below
Outputs:
- d_queries: bfloat16 [32768, 1024], P(('ctx', 'head'))
- d_keys: bfloat16 [32768, 1024], P(('ctx', 'head'))
- d_values: bfloat16 [32768, 1024], P(('ctx', 'head'))
Inputs may be any that keep to these rules, and one draw needn't show every extreme that they name: `pair_blocks`: entry 0 of row b is b itself; every entry of row b is a block of a person within 2 persons of the person of block b (a person's tokens are 512 in a row). Entries may repeat. Only the first pair_count[b] entries of row b are listed.
All inputs are finite; a program needn't handle non-finite values.
Results may differ from a plain program's by a relative error of at most 0.012.
The roundings to bfloat16 on the way count: a program that leaves them out, or rounds other values in their place, can miss the bound.
Values may be sent and summed in bfloat16 or wider, within the bound.
A program may use at most 192 MiB of HBM per device.

v0:
```python
import jax
import jax.numpy as jnp
from jax import lax
from jax.sharding import PartitionSpec as P

HEAD_DIM = 64
BLOCK = 64
REACH = 2
masked_value = -1e30


def shifted(shard, axis, by):
    peers = lax.axis_size(axis)
    pairs = [(i, i + by) for i in range(peers) if 0 <= i + by < peers]
    return lax.ppermute(shard, axis, pairs)


def expand_mask(block_mask, block_rows):
    count_rows, count_cols = block_mask.shape
    widened = jnp.broadcast_to(
        block_mask[:, None, :, None], (count_rows, block_rows, count_cols, block_rows)
    )
    return widened.reshape(count_rows * block_rows, count_cols * block_rows)


def block_listing(pair_blocks, pair_count, first_query, query_blocks, first_key, key_blocks):
    lists = lax.dynamic_slice_in_dim(pair_blocks, first_query, query_blocks, 0)
    counts = lax.dynamic_slice_in_dim(pair_count, first_query, query_blocks, 0)
    live_slots = jnp.arange(lists.shape[1], dtype=jnp.int32)[None, :] < counts[:, None]
    wanted = first_key + jnp.arange(key_blocks, dtype=jnp.int32)
    return jnp.any((lists[:, :, None] == wanted[None, None, :]) & live_slots[:, :, None], axis=1)


def masked_scores(query_heads, key_heads, token_mask, score_scale):
    product = jnp.einsum("qhd,khd->hqk", query_heads, key_heads, preferred_element_type=jnp.float32)
    return jnp.where(token_mask[None], product * score_scale, masked_value)


def score_grads(probs, dout_heads, value_heads, row_delta):
    d_probs = jnp.einsum(
        "qhd,khd->hqk", dout_heads, value_heads, preferred_element_type=jnp.float32
    )
    return (probs * (d_probs - row_delta[:, :, None])).astype(jnp.bfloat16)


def key_value_grads(d_scores, probs, query_heads, dout_heads):
    key_part = jnp.einsum("hqk,qhd->khd", d_scores, query_heads, preferred_element_type=jnp.float32)
    value_part = jnp.einsum(
        "hqk,qhd->khd", probs.astype(jnp.bfloat16), dout_heads, preferred_element_type=jnp.float32
    )
    return jnp.stack([key_part, value_part]).astype(jnp.bfloat16)


def widen_part(rounded):
    return lax.optimization_barrier(rounded).astype(jnp.float32)


def on_device(queries, keys_in, values, d_out, pair_blocks, pair_count):
    entering = jnp.stack([queries, keys_in, values, d_out])
    head_local = lax.all_to_all(entering, "head", split_axis=2, concat_axis=1, tiled=True)
    frames = head_local.shape[1]
    feature_cols = head_local.shape[2]
    heads_dev = feature_cols // HEAD_DIM
    blocks_dev = frames // BLOCK
    window_span = 2 * REACH + 1
    score_scale = HEAD_DIM ** (-0.5)
    position = lax.axis_index("ctx")

    def split_heads(matrix):
        return matrix.reshape(frames, heads_dev, HEAD_DIM)

    query_heads = split_heads(head_local[0])
    dout_heads = split_heads(head_local[3])
    window_mask = block_listing(
        pair_blocks,
        pair_count,
        position * blocks_dev,
        blocks_dev,
        (position - REACH) * blocks_dev,
        window_span * blocks_dev,
    )
    key_pair = head_local[1:3]
    remote_tiles = {0: key_pair}
    for direction in (1, -1):
        current = key_pair
        for stride in range(1, REACH + 1):
            current = shifted(current, "ctx", direction)
            remote_tiles[-direction * stride] = current
    offsets = [0]
    for stride in range(1, REACH + 1):
        offsets = offsets + [-stride, stride]
    tile_masks = {}
    for offset in offsets:
        column = (offset + REACH) * blocks_dev
        tile_masks[offset] = expand_mask(window_mask[:, column : column + blocks_dev], BLOCK)
    row_top = jnp.full((heads_dev, frames), masked_value, jnp.float32)
    row_total = jnp.zeros((heads_dev, frames), jnp.float32)
    tile_scores = {}
    for offset in offsets:
        scores = masked_scores(
            query_heads, split_heads(remote_tiles[offset][0]), tile_masks[offset], score_scale
        )
        tile_scores[offset] = scores
        new_top = jnp.maximum(row_top, jnp.max(scores, axis=-1))
        kept = jnp.where(tile_masks[offset][None], jnp.exp(scores - new_top[:, :, None]), 0.0)
        row_total = row_total * jnp.exp(row_top - new_top) + jnp.sum(kept, axis=-1)
        row_top = new_top
    log_total = row_top + jnp.log(row_total)
    attention = jnp.zeros((frames, heads_dev, HEAD_DIM), jnp.float32)
    tile_probs = {}
    for offset in offsets:
        probs = jnp.where(
            tile_masks[offset][None], jnp.exp(tile_scores[offset] - log_total[:, :, None]), 0.0
        )
        tile_probs[offset] = probs
        attention = attention + jnp.einsum(
            "hqk,khd->qhd",
            probs.astype(jnp.bfloat16),
            split_heads(remote_tiles[offset][1]),
            preferred_element_type=jnp.float32,
        )
    row_delta = jnp.sum(dout_heads.astype(jnp.float32) * attention, axis=-1).T
    query_grad = jnp.zeros((frames, heads_dev, HEAD_DIM), jnp.float32)
    tile_parts = {}
    for offset in offsets:
        key_heads = split_heads(remote_tiles[offset][0])
        d_scores = score_grads(
            tile_probs[offset], dout_heads, split_heads(remote_tiles[offset][1]), row_delta
        )
        query_grad = query_grad + jnp.einsum(
            "hqk,khd->qhd", d_scores, key_heads, preferred_element_type=jnp.float32
        )
        tile_parts[offset] = key_value_grads(d_scores, tile_probs[offset], query_heads, dout_heads)
    collected = widen_part(tile_parts[0])
    for offset in offsets[1:]:
        arrived = shifted(tile_parts[offset], "ctx", offset)
        collected = collected + arrived.astype(jnp.float32)
    query_out = (query_grad * score_scale).astype(jnp.bfloat16).reshape(frames, feature_cols)
    key_out = (collected[0] * score_scale).astype(jnp.bfloat16).reshape(frames, feature_cols)
    value_out = collected[1].astype(jnp.bfloat16).reshape(frames, feature_cols)
    leaving = lax.all_to_all(
        jnp.stack([query_out, key_out, value_out]), "head", split_axis=1, concat_axis=2, tiled=True
    )
    return (leaving[0], leaving[1], leaving[2])


def solution(mesh):
    placed = (
        P(("ctx", "head"), None),
        P(("ctx", "head"), None),
        P(("ctx", "head"), None),
        P(("ctx", "head"), None),
        P(),
        P(),
    )
    return jax.shard_map(
        on_device,
        mesh=mesh,
        in_specs=placed,
        out_specs=(P(("ctx", "head"), None), P(("ctx", "head"), None), P(("ctx", "head"), None)),
        check_vma=False,
    )
```

profile of v0, /device:TPU:121, one launch (start us, length us, event | category | flops | bytes accessed | tf_op | source)
XLA Modules:
  0.0 277.8 jit_solution(14616400120939298782)
XLA Ops:
  0.6 1.8 pad_maximum_fusion
  2.4 2.6 copy.108
  5.0 4.0 %all-to-all-start = ((bf16[4,256,1024]{1,0,2:T(4,128)(2,1)}), bf16[4,256,1024]{1,0,2:T(4,128)(2,1)S(1)}, u32[]{:S(2)}, u32[]{:S(2)}) async-start(bf16[4,256,1024]{1,0,2:T(4,128)(2,1)} %copy.108), calls=%async_computation | async-start | bytes 4194304 | tf_op jit(solution)/shard_map/all_to_all | solution.py:60
  10.0 24.4 %all-to-all-done = bf16[4,256,1024]{1,0,2:T(4,128)(2,1)S(1)} async-done(((bf16[4,256,1024]{1,0,2:T(4,128)(2,1)}), bf16[4,256,1024]{1,0,2:T(4,128)(2,1)S(1)}, u32[]{:S(2)}, u32[]{:S(2)}) %all-to-all-start) | async-done | bytes 2097184 | tf_op jit(solution)/shard_map/all_to_all | solution.py:60
  34.5 1.3 copy-done.5
  35.8 3.7 %copy.176 = bf16[4,256,2,512]{1,2,3,0:T(2,128)(2,1)S(1)} copy(bf16[4,256,2,512]{1,0,3,2:T(4,128)(2,1)} %bitcast.163) | data formatting | bytes 4194304 | tf_op jit(solution)/shard_map/all_to_all | solution.py:60
  40.3 1.5 slice.97
  41.8 3.8 %collective-permute-start.1 = (bf16[2,512,512]{1,2,0:T(8,128)(2,1)}, bf16[2,512,512]{1,2,0:T(8,128)(2,1)}, u32[]{:S(2)}, u32[]{:S(2)}) collective-permute-start(bf16[2,512,512]{1,2,0:T(8,128)(2,1)} %slice.97), channel_id=1, source_target_pairs={{2,0},{4,2},{6,4},{8,6},{10,8},{12,10},{14,12},{16,14},{18,16},{20... | collective-permute-start | bytes 3145736 | tf_op jit(solution)/shard_map/ppermute | solution.py:15
  45.7 6.2 %collective-permute-start = (bf16[2,512,512]{1,2,0:T(8,128)(2,1)}, bf16[2,512,512]{1,2,0:T(8,128)(2,1)}, u32[]{:S(2)}, u32[]{:S(2)}) collective-permute-start(bf16[2,512,512]{1,2,0:T(8,128)(2,1)} %slice.97), channel_id=1, source_target_pairs={{0,2},{2,4},{4,6},{6,8},{8,10},{10,12},{12,14},{14,16},{16,18},{18... | collective-permute-start | bytes 3145736 | tf_op jit(solution)/shard_map/ppermute | solution.py:15
  56.0 1.8 broadcast_in_dim.150
  58.9 1.8 broadcast_in_dim.145
  60.7 2.4 fusion.44
  63.1 1.4 reshape_squeeze.52
  64.5 1.4 reshape_squeeze.47
  65.9 1.4 reshape_squeeze.46
  67.2 2.2 reshape_squeeze.53
  69.4 1.5 fusion.5
  70.9 1.9 collective-permute-start.3
  72.8 1.3 fusion.46
  74.1 8.1 %collective-permute-start.2 = (bf16[2,512,512]{1,2,0:T(8,128)(2,1)}, bf16[2,512,512]{1,2,0:T(8,128)(2,1)S(1)}, u32[]{:S(2)}, u32[]{:S(2)}) collective-permute-start(bf16[2,512,512]{1,2,0:T(8,128)(2,1)} %collective-permute-done), channel_id=1, source_target_pairs={{0,2},{2,4},{4,6},{6,8},{8,10},{10,12},{12,14},{14,16},{16,18},{18... | collective-permute-start | bytes 3145736 | tf_op jit(solution)/shard_map/ppermute | solution.py:15
  82.3 1.3 fusion.47
  83.5 1.5 fusion.7
  85.0 1.5 fusion.6
  86.5 4.9 %collective-permute-done.3 = bf16[2,512,512]{1,2,0:T(8,128)(2,1)S(1)} collective-permute-done((bf16[2,512,512]{1,2,0:T(8,128)(2,1)}, bf16[2,512,512]{1,2,0:T(8,128)(2,1)S(1)}, u32[]{:S(2)}, u32[]{:S(2)}) %collective-permute-start.3) | collective-permute-done | bytes 1048608 | tf_op jit(solution)/shard_map/ppermute | solution.py:15
  91.5 4.7 %fusion.9 = (f32[8,512]{1,0:T(8,128)S(1)}, f32[8,512,512]{1,2,0:T(8,128)}) fusion(pred[512,512]{0,1:T(8,128)(4,1)S(1)} %broadcast_in_dim.159, bf16[512,8,64]{0,2,1:T(8,128)(2,1)S(1)} %reshape_squeeze.47, bf16[512,8,64]{0,2,1:T(8,128)(2,1)S(1)} %bitcast.170), kind=kOutput, calls=%fused_computation.29 | convolution fusion | flops 274722816 | bytes 9715712 | tf_op jit(solution)/shard_map/qhd,khd->hqk/dot_general | solution.py:35
  96.3 4.7 %fusion.8 = (f32[8,512]{1,0:T(8,128)S(1)}, f32[8,512,512]{1,2,0:T(8,128)}) fusion(pred[512,512]{0,1:T(8,128)(4,1)S(1)} %broadcast_in_dim.156, bf16[512,8,64]{0,2,1:T(8,128)(2,1)S(1)} %reshape_squeeze.47, bf16[512,8,64]{0,2,1:T(8,128)(2,1)S(1)} %bitcast.164), kind=kOutput, calls=%fused_computation.28 | convolution fusion | flops 274722816 | bytes 9715712 | tf_op jit(solution)/shard_map/qhd,khd->hqk/dot_general | solution.py:35
  101.1 2.5 select_reduce_fusion.4
  103.6 7.9 %select_reduce_fusion = (f32[8,512]{1,0:T(8,128)S(1)}, f32[8,512]{1,0:T(8,128)S(1)}) fusion(f32[8,512,512]{1,2,0:T(8,128)} %get-tuple-element.29, f32[8,512]{1,0:T(8,128)S(1)} %get-tuple-element.3, pred[512,512]{0,1:T(8,128)(4,1)S(1)} %broadcast_in_dim.159, f32[8,512]{1,0:T(8,128)S(1)} %get-tuple-element.4, f32[8,512,512]{1,2,0:T(8,128)} %get-tuple-element.31, ...), kind=kLoop, calls=%fused_computation.10 | loop fusion | flops 20963328 | bytes 17367040 | tf_op jit(solution)/shard_map/reduce_sum | solution.py:106
  111.5 4.0 %select_reduce_fusion.2 = (f32[8,512]{1,0:T(8,128)S(1)}, f32[8,512]{1,0:T(8,128)S(1)}) fusion(f32[8,512,512]{1,2,0:T(8,128)S(1)} %get-tuple-element.33, f32[8,512]{1,0:T(8,128)S(1)} %get-tuple-element.5, pred[512,512]{0,1:T(8,128)(4,1)S(1)} %broadcast_in_dim.153, f32[8,512]{1,0:T(8,128)S(1)} %get-tuple-element.6, f32[8,512,512]{1,2,0:T(8,128)S(1)} %get-tuple-element.35, ...), kind=kLoop, calls=%fused_computation.12 | loop fusion | flops 20963328 | bytes 17367040 | tf_op jit(solution)/shard_map/reduce_sum | solution.py:106
  115.5 6.5 %fusion.26 = bf16[1,512,8,64]{1,3,2,0:T(8,128)(2,1)} fusion(bf16[512,8,64]{0,2,1:T(8,128)(2,1)S(1)} %reshape_squeeze.52, f32[8,512,512]{1,2,0:T(8,128)} %get-tuple-element.29, f32[8,512]{1,0:T(8,128)S(1)} %log_add_fusion, pred[512,512]{0,1:T(8,128)(4,1)S(1)} %broadcast_in_dim.159), kind=kOutput, calls=%fused_computation.66 | convolution fusion | flops 279183360 | bytes 9715712 | tf_op jit(solution)/shard_map/hqk,qhd->khd/dot_general | solution.py:48
  122.0 6.5 %fusion.24 = bf16[1,512,8,64]{1,3,2,0:T(8,128)(2,1)} fusion(bf16[512,8,64]{0,2,1:T(8,128)(2,1)S(1)} %reshape_squeeze.52, f32[8,512,512]{1,2,0:T(8,128)} %get-tuple-element.31, f32[8,512]{1,0:T(8,128)S(1)} %log_add_fusion, pred[512,512]{0,1:T(8,128)(4,1)S(1)} %broadcast_in_dim.156), kind=kOutput, calls=%fused_computation.64 | convolution fusion | flops 279183360 | bytes 9715712 | tf_op jit(solution)/shard_map/hqk,qhd->khd/dot_general | solution.py:48
  128.5 5.8 %fusion.36 = f32[8,64,512]{2,1,0:T(8,128)S(1)} fusion(bf16[512,8,64]{0,2,1:T(8,128)(2,1)S(1)} %bitcast.185, f32[8,512,512]{1,2,0:T(8,128)} %get-tuple-element.29, f32[8,512]{1,0:T(8,128)S(1)} %log_add_fusion, pred[512,512]{0,1:T(8,128)(4,1)S(1)} %broadcast_in_dim.159), kind=kOutput, calls=%fused_computation.82 | convolution fusion | flops 278921216 | bytes 10240000 | tf_op jit(solution)/shard_map/hqk,khd->qhd/dot_general | solution.py:116
  134.3 2.6 fusion.39
  136.8 2.4 convolution_add_fusion.5
  139.3 2.4 convolution_add_fusion.4
  141.8 5.9 %fusion.16 = f32[512,8]{0,1:T(8,128)S(1)} fusion(f32[8,64,512]{2,1,0:T(8,128)S(1)} %fusion.36, f32[8,64,512]{2,1,0:T(8,128)S(1)} %convolution_add_fusion.4, bf16[512,8,64]{0,2,1:T(8,128)(2,1)S(1)} %bitcast.187, bf16[512,8,64]{0,2,1:T(8,128)(2,1)S(1)} %reshape_squeeze.52, f32[8,512,512]{1,2,0:T(8,128)} %get-tuple-element.31, f32[8,512]{1,0:T(8,128)S(1)} %log_add_fusion, ...), kind=kOutput, calls=%fused_computation.56 | convolution fusion | flops 280227840 | bytes 11829248 | tf_op jit(solution)/shard_map/hqk,khd->qhd/dot_general | solution.py:116
  147.7 6.8 %multiply_convert_fusion = bf16[8,512,512]{1,2,0:T(8,128)(2,1)} fusion(f32[8,512,512]{1,2,0:T(8,128)} %get-tuple-element.29, f32[8,512]{1,0:T(8,128)S(1)} %bitcast.193, f32[8,512]{1,0:T(8,128)S(1)} %log_add_fusion, pred[512,512]{0,1:T(8,128)(4,1)S(1)} %broadcast_in_dim.159, bf16[512,8,64]{0,2,1:T(8,128)(2,1)S(1)} %reshape_squeeze.52, ...), kind=kOutput, calls=%fused_computation | convolution fusion | flops 283115520 | bytes 13926400 | tf_op jit(solution)/shard_map/qhd,khd->hqk/dot_general | solution.py:40
  154.5 6.8 %multiply_convert_fusion.1 = bf16[8,512,512]{1,2,0:T(8,128)(2,1)} fusion(f32[8,512,512]{1,2,0:T(8,128)} %get-tuple-element.31, f32[8,512]{1,0:T(8,128)S(1)} %bitcast.194, f32[8,512]{1,0:T(8,128)S(1)} %log_add_fusion, pred[512,512]{0,1:T(8,128)(4,1)S(1)} %broadcast_in_dim.156, bf16[512,8,64]{0,2,1:T(8,128)(2,1)S(1)} %reshape_squeeze.52, ...), kind=kOutput, calls=%fused_computation.1 | convolution fusion | flops 283115520 | bytes 13926400 | tf_op jit(solution)/shard_map/qhd,khd->hqk/dot_general | solution.py:40
  161.3 3.3 %fusion.22 = bf16[1,512,8,64]{1,3,2,0:T(8,128)(2,1)} fusion(bf16[512,8,64]{0,2,1:T(8,128)(2,1)S(1)} %reshape_squeeze.52, f32[8,512,512]{1,2,0:T(8,128)S(1)} %get-tuple-element.33, f32[8,512]{1,0:T(8,128)S(1)} %log_add_fusion, pred[512,512]{0,1:T(8,128)(4,1)S(1)} %broadcast_in_dim.153), kind=kOutput, calls=%fused_computation.62 | convolution fusion | flops 279183360 | bytes 9715712 | tf_op jit(solution)/shard_map/hqk,qhd->khd/dot_general | solution.py:48
  164.6 4.8 %multiply_convert_fusion.2 = bf16[8,512,512]{1,2,0:T(8,128)(2,1)} fusion(f32[8,512,512]{1,2,0:T(8,128)S(1)} %get-tuple-element.33, f32[8,512]{1,0:T(8,128)S(1)} %bitcast.195, f32[8,512]{1,0:T(8,128)S(1)} %log_add_fusion, pred[512,512]{0,1:T(8,128)(4,1)S(1)} %broadcast_in_dim.153, bf16[512,8,64]{0,2,1:T(8,128)(2,1)S(1)} %reshape_squeeze.52, ...), kind=kOutput, calls=%fused_computation.2 | convolution fusion | flops 283115520 | bytes 13926400 | tf_op jit(solution)/shard_map/qhd,khd->hqk/dot_general | solution.py:40
  169.4 3.3 %fusion.20 = bf16[1,512,8,64]{1,3,2,0:T(8,128)(2,1)} fusion(bf16[512,8,64]{0,2,1:T(8,128)(2,1)S(1)} %reshape_squeeze.52, f32[8,512,512]{1,2,0:T(8,128)S(1)} %get-tuple-element.35, f32[8,512]{1,0:T(8,128)S(1)} %log_add_fusion, pred[512,512]{0,1:T(8,128)(4,1)S(1)} %broadcast_in_dim.150), kind=kOutput, calls=%fused_computation.60 | convolution fusion | flops 279183360 | bytes 9715712 | tf_op jit(solution)/shard_map/hqk,qhd->khd/dot_general | solution.py:48
  172.7 3.4 %multiply_convert_fusion.3 = bf16[8,512,512]{1,2,0:T(8,128)(2,1)S(1)} fusion(f32[8,512,512]{1,2,0:T(8,128)S(1)} %get-tuple-element.35, f32[8,512]{1,0:T(8,128)S(1)} %bitcast.196, f32[8,512]{1,0:T(8,128)S(1)} %log_add_fusion, pred[512,512]{0,1:T(8,128)(4,1)S(1)} %broadcast_in_dim.150, bf16[512,8,64]{0,2,1:T(8,128)(2,1)S(1)} %reshape_squeeze.52, ...), kind=kOutput, calls=%fused_computation.3 | convolution fusion | flops 283115520 | bytes 13926400 | tf_op jit(solution)/shard_map/qhd,khd->hqk/dot_general | solution.py:40
  176.1 2.5 fusion.18
  178.6 3.4 %multiply_convert_fusion.4 = bf16[8,512,512]{1,2,0:T(8,128)(2,1)S(1)} fusion(f32[8,512,512]{1,2,0:T(8,128)S(1)} %get-tuple-element.37, f32[8,512]{1,0:T(8,128)S(1)} %bitcast.197, f32[8,512]{1,0:T(8,128)S(1)} %log_add_fusion, pred[512,512]{0,1:T(8,128)(4,1)S(1)} %broadcast_in_dim.145, bf16[512,8,64]{0,2,1:T(8,128)(2,1)S(1)} %reshape_squeeze.52, ...), kind=kOutput, calls=%fused_computation.4 | convolution fusion | flops 283115520 | bytes 13926400 | tf_op jit(solution)/shard_map/qhd,khd->hqk/dot_general | solution.py:40
  182.1 1.4 fusion.17
  184.4 1.4 fusion.25
  185.8 1.1 pad_maximum_fusion.6
  186.8 1.9 collective-permute-start.7
  188.8 1.4 fusion.23
  190.2 1.1 pad_maximum_fusion.5
  191.3 3.6 %collective-permute-start.6 = (bf16[2,512,8,64]{1,3,2,0:T(8,128)(2,1)}, bf16[2,512,8,64]{1,3,2,0:T(8,128)(2,1)}, u32[]{:S(2)}, u32[]{:S(2)}) collective-permute-start(bf16[2,512,8,64]{1,3,2,0:T(8,128)(2,1)} %pad_maximum_fusion.5), channel_id=1, source_target_pairs={{4,0},{6,2},{8,4},{10,6},{12,8},{14,10},{16,12},{18,14},{20,16},{2... | collective-permute-start | bytes 3145736 | tf_op jit(solution)/shard_map/ppermute | solution.py:15
  194.9 1.4 fusion.21
  196.3 1.1 pad_maximum_fusion.4
  197.3 11.0 %collective-permute-start.5 = (bf16[2,512,8,64]{1,3,2,0:T(8,128)(2,1)}, bf16[2,512,8,64]{1,3,2,0:T(8,128)(2,1)}, u32[]{:S(2)}, u32[]{:S(2)}) collective-permute-start(bf16[2,512,8,64]{1,3,2,0:T(8,128)(2,1)} %pad_maximum_fusion.4), channel_id=1, source_target_pairs={{0,2},{2,4},{4,6},{6,8},{8,10},{10,12},{12,14},{14,16},{16,18},{18... | collective-permute-start | bytes 3145736 | tf_op jit(solution)/shard_map/ppermute | solution.py:15
  208.4 1.4 fusion.19
  209.8 1.1 pad_maximum_fusion.3
  210.9 1.9 collective-permute-start.4
  217.6 5.7 %collective-permute-done.5 = bf16[2,512,8,64]{1,3,2,0:T(8,128)(2,1)} collective-permute-done((bf16[2,512,8,64]{1,3,2,0:T(8,128)(2,1)}, bf16[2,512,8,64]{1,3,2,0:T(8,128)(2,1)}, u32[]{:S(2)}, u32[]{:S(2)}) %collective-permute-start.5) | collective-permute-done | bytes 1048608 | tf_op jit(solution)/shard_map/ppermute | solution.py:15
  223.3 10.5 %collective-permute-done.4 = bf16[2,512,8,64]{1,3,2,0:T(8,128)(2,1)} collective-permute-done((bf16[2,512,8,64]{1,3,2,0:T(8,128)(2,1)}, bf16[2,512,8,64]{1,3,2,0:T(8,128)(2,1)}, u32[]{:S(2)}, u32[]{:S(2)}) %collective-permute-start.4) | collective-permute-done | bytes 1048608 | tf_op jit(solution)/shard_map/ppermute | solution.py:15
  233.8 3.0 %convert_add_fusion = f32[2,512,8,64]{1,3,2,0:T(8,128)S(1)} fusion(bf16[2,512,8,64]{1,3,2,0:T(8,128)(2,1)} %collective-permute-done.7, bf16[2,512,8,64]{1,3,2,0:T(8,128)(2,1)} %collective-permute-done.6, bf16[2,512,8,64]{1,3,2,0:T(8,128)(2,1)} %collective-permute-done.5, bf16[2,512,8,64]{1,3,2,0:T(8,128)(2,1)} %collective-permute-done.4, ...), kind=kLoop, calls=%fused_computation.33 | loop fusion | flops 4718592 | bytes 7340032 | tf_op jit(solution)/shard_map/add | solution.py:137
  238.7 2.4 copy.142
  241.1 3.6 %pad_maximum_fusion.1 = bf16[3,512,512]{2,0,1:T(4,128)(2,1)S(1)} fusion(bf16[1,512,512]{2,0,1:T(2,128)(2,1)S(1)} %copy.143, bf16[1,512,512]{2,0,1:T(2,128)(2,1)S(1)} %copy.142, bf16[1,512,512]{2,0,1:T(2,128)(2,1)S(1)} %copy.141), kind=kLoop, calls=%fused_computation.31 | loop fusion | flops 4718592 | bytes 3145728 | tf_op jit(solution)/shard_map/stack | solution.py:142
  244.7 25.3 %all_to_all.30 = bf16[3,512,512]{2,0,1:T(4,128)(2,1)S(1)} all-to-all(bf16[3,512,512]{2,0,1:T(4,128)(2,1)S(1)} %pad_maximum_fusion.1), channel_id=1, replica_groups=mesh['ctx'=64,'head'=2] {'head'}, dimensions={1} | all-to-all | bytes 3145728 | tf_op jit(solution)/shard_map/all_to_all | solution.py:141
  270.0 2.2 fusion.43
  (81 shorter events, 19.7 us)
Async XLA Ops:
  0.6 8.4 %copy-start = (s32[512,16]{0,1:T(8,128)S(1)}, s32[512,16]{0,1:T(8,128)}, u32[]{:S(2)}) copy-start(s32[512,16]{0,1:T(8,128)} %param.10) | copy-start | bytes 98308
  5.0 29.4 %all-to-all-start = ((bf16[4,256,1024]{1,0,2:T(4,128)(2,1)}), bf16[4,256,1024]{1,0,2:T(4,128)(2,1)S(1)}, u32[]{:S(2)}, u32[]{:S(2)}) async-start(bf16[4,256,1024]{1,0,2:T(4,128)(2,1)} %copy.108), calls=%async_computation | async-start | bytes 4194304 | tf_op jit(solution)/shard_map/all_to_all | solution.py:60
  34.5 1.3 copy-start.5
  41.8 29.1 %collective-permute-start.1 = (bf16[2,512,512]{1,2,0:T(8,128)(2,1)}, bf16[2,512,512]{1,2,0:T(8,128)(2,1)}, u32[]{:S(2)}, u32[]{:S(2)}) collective-permute-start(bf16[2,512,512]{1,2,0:T(8,128)(2,1)} %slice.97), channel_id=1, source_target_pairs={{2,0},{4,2},{6,4},{8,6},{10,8},{12,10},{14,12},{16,14},{18,16},{20... | collective-permute-start | bytes 3145736 | tf_op jit(solution)/shard_map/ppermute | solution.py:15
  45.7 28.4 %collective-permute-start = (bf16[2,512,512]{1,2,0:T(8,128)(2,1)}, bf16[2,512,512]{1,2,0:T(8,128)(2,1)}, u32[]{:S(2)}, u32[]{:S(2)}) collective-permute-start(bf16[2,512,512]{1,2,0:T(8,128)(2,1)} %slice.97), channel_id=1, source_target_pairs={{0,2},{2,4},{4,6},{6,8},{8,10},{10,12},{12,14},{14,16},{16,18},{18... | collective-permute-start | bytes 3145736 | tf_op jit(solution)/shard_map/ppermute | solution.py:15
  70.9 20.5 %collective-permute-start.3 = (bf16[2,512,512]{1,2,0:T(8,128)(2,1)}, bf16[2,512,512]{1,2,0:T(8,128)(2,1)S(1)}, u32[]{:S(2)}, u32[]{:S(2)}) collective-permute-start(bf16[2,512,512]{1,2,0:T(8,128)(2,1)} %collective-permute-done.1), channel_id=1, source_target_pairs={{2,0},{4,2},{6,4},{8,6},{10,8},{12,10},{14,12},{16,14},{18,16},{20... | collective-permute-start | bytes 3145736 | tf_op jit(solution)/shard_map/ppermute | solution.py:15
  74.1 65.2 %copy-start.8 = (bf16[1,512,512]{1,2,0:T(8,128)(2,1)}, bf16[1,512,512]{1,2,0:T(8,128)(2,1)S(1)}, u32[]{:S(2)}) copy-start(bf16[1,512,512]{1,2,0:T(8,128)(2,1)S(1)} %get-tuple-element.16) | copy-start | bytes 1572868
  74.1 22.1 %collective-permute-start.2 = (bf16[2,512,512]{1,2,0:T(8,128)(2,1)}, bf16[2,512,512]{1,2,0:T(8,128)(2,1)S(1)}, u32[]{:S(2)}, u32[]{:S(2)}) collective-permute-start(bf16[2,512,512]{1,2,0:T(8,128)(2,1)} %collective-permute-done), channel_id=1, source_target_pairs={{0,2},{2,4},{4,6},{6,8},{8,10},{10,12},{12,14},{14,16},{16,18},{18... | collective-permute-start | bytes 3145736 | tf_op jit(solution)/shard_map/ppermute | solution.py:15
  83.5 53.3 %copy-start.10 = (bf16[1,512,512]{1,2,0:T(8,128)(2,1)}, bf16[1,512,512]{1,2,0:T(8,128)(2,1)S(1)}, u32[]{:S(2)}) copy-start(bf16[1,512,512]{1,2,0:T(8,128)(2,1)S(1)} %get-tuple-element.18) | copy-start | bytes 1572868
  91.5 37.0 %copy-start.12 = (bf16[1,512,512]{1,2,0:T(8,128)(2,1)}, bf16[1,512,512]{1,2,0:T(8,128)(2,1)S(1)}, u32[]{:S(2)}) copy-start(bf16[1,512,512]{1,2,0:T(8,128)(2,1)S(1)} %get-tuple-element.20) | copy-start | bytes 1572868
  96.3 45.4 %copy-start.13 = (bf16[1,512,512]{1,2,0:T(8,128)(2,1)}, bf16[1,512,512]{1,2,0:T(8,128)(2,1)S(1)}, u32[]{:S(2)}) copy-start(bf16[1,512,512]{1,2,0:T(8,128)(2,1)S(1)} %get-tuple-element.14) | copy-start | bytes 1572868
  128.5 5.8 %copy-start.6 = (bf16[512,8,64]{0,2,1:T(8,128)(2,1)S(1)}, bf16[512,8,64]{0,2,1:T(8,128)(2,1)}, u32[]{:S(2)}) copy-start(bf16[512,8,64]{0,2,1:T(8,128)(2,1)} %reshape_squeeze.53) | copy-start | bytes 1572868
  161.3 3.3 %copy-start.9 = (bf16[1,512,512]{1,2,0:T(8,128)(2,1)S(1)}, bf16[1,512,512]{1,2,0:T(8,128)(2,1)}, u32[]{:S(2)}) copy-start(bf16[1,512,512]{1,2,0:T(8,128)(2,1)} %copy-done.8) | copy-start | bytes 1572868
  169.4 3.3 %copy-start.11 = (bf16[1,512,512]{1,2,0:T(8,128)(2,1)S(1)}, bf16[1,512,512]{1,2,0:T(8,128)(2,1)}, u32[]{:S(2)}) copy-start(bf16[1,512,512]{1,2,0:T(8,128)(2,1)} %copy-done.10) | copy-start | bytes 1572868
  176.1 2.5 copy-start.7
  182.1 2.3 copy-start.3
  182.1 3.7 %copy-start.15 = (bf16[1,512,8,64]{1,3,2,0:T(8,128)(2,1)S(1)}, bf16[1,512,8,64]{1,3,2,0:T(8,128)(2,1)}, u32[]{:S(2)}) copy-start(bf16[1,512,8,64]{1,3,2,0:T(8,128)(2,1)} %fusion.26) | copy-start | bytes 1572868
  182.1 6.7 %copy-start.2 = (bf16[8,512,512]{1,2,0:T(8,128)(2,1)S(1)}, bf16[8,512,512]{1,2,0:T(8,128)(2,1)}, u32[]{:S(2)}) copy-start(bf16[8,512,512]{1,2,0:T(8,128)(2,1)} %multiply_convert_fusion.1) | copy-start | bytes 12582916
  183.5 6.7 %copy-start.14 = (bf16[1,512,8,64]{1,3,2,0:T(8,128)(2,1)S(1)}, bf16[1,512,8,64]{1,3,2,0:T(8,128)(2,1)}, u32[]{:S(2)}) copy-start(bf16[1,512,8,64]{1,3,2,0:T(8,128)(2,1)} %fusion.24) | copy-start | bytes 1572868
  184.4 10.5 %copy-start.4 = (bf16[8,512,512]{1,2,0:T(8,128)(2,1)S(1)}, bf16[8,512,512]{1,2,0:T(8,128)(2,1)}, u32[]{:S(2)}) copy-start(bf16[8,512,512]{1,2,0:T(8,128)(2,1)} %multiply_convert_fusion.2) | copy-start | bytes 12582916
  185.8 10.5 %copy-start.17 = (bf16[1,512,8,64]{1,3,2,0:T(8,128)(2,1)S(1)}, bf16[1,512,8,64]{1,3,2,0:T(8,128)(2,1)}, u32[]{:S(2)}) copy-start(bf16[1,512,8,64]{1,3,2,0:T(8,128)(2,1)} %fusion.22) | copy-start | bytes 1572868
  186.8 30.2 %collective-permute-start.7 = (bf16[2,512,8,64]{1,3,2,0:T(8,128)(2,1)}, bf16[2,512,8,64]{1,3,2,0:T(8,128)(2,1)}, u32[]{:S(2)}, u32[]{:S(2)}) collective-permute-start(bf16[2,512,8,64]{1,3,2,0:T(8,128)(2,1)} %pad_maximum_fusion.6), channel_id=1, source_target_pairs={{0,4},{2,6},{4,8},{6,10},{8,12},{10,14},{12,16},{14,18},{16,20},{1... | collective-permute-start | bytes 3145736 | tf_op jit(solution)/shard_map/ppermute | solution.py:15
  190.2 19.6 %copy-start.16 = (bf16[1,512,8,64]{1,3,2,0:T(8,128)(2,1)S(1)}, bf16[1,512,8,64]{1,3,2,0:T(8,128)(2,1)}, u32[]{:S(2)}) copy-start(bf16[1,512,8,64]{1,3,2,0:T(8,128)(2,1)} %fusion.20) | copy-start | bytes 1572868
  191.3 26.3 %collective-permute-start.6 = (bf16[2,512,8,64]{1,3,2,0:T(8,128)(2,1)}, bf16[2,512,8,64]{1,3,2,0:T(8,128)(2,1)}, u32[]{:S(2)}, u32[]{:S(2)}) collective-permute-start(bf16[2,512,8,64]{1,3,2,0:T(8,128)(2,1)} %pad_maximum_fusion.5), channel_id=1, source_target_pairs={{4,0},{6,2},{8,4},{10,6},{12,8},{14,10},{16,12},{18,14},{20,16},{2... | collective-permute-start | bytes 3145736 | tf_op jit(solution)/shard_map/ppermute | solution.py:15
  197.3 25.9 %collective-permute-start.5 = (bf16[2,512,8,64]{1,3,2,0:T(8,128)(2,1)}, bf16[2,512,8,64]{1,3,2,0:T(8,128)(2,1)}, u32[]{:S(2)}, u32[]{:S(2)}) collective-permute-start(bf16[2,512,8,64]{1,3,2,0:T(8,128)(2,1)} %pad_maximum_fusion.4), channel_id=1, source_target_pairs={{0,2},{2,4},{4,6},{6,8},{8,10},{10,12},{12,14},{14,16},{16,18},{18... | collective-permute-start | bytes 3145736 | tf_op jit(solution)/shard_map/ppermute | solution.py:15
  210.9 22.9 %collective-permute-start.4 = (bf16[2,512,8,64]{1,3,2,0:T(8,128)(2,1)}, bf16[2,512,8,64]{1,3,2,0:T(8,128)(2,1)}, u32[]{:S(2)}, u32[]{:S(2)}) collective-permute-start(bf16[2,512,8,64]{1,3,2,0:T(8,128)(2,1)} %pad_maximum_fusion.3), channel_id=1, source_target_pairs={{2,0},{4,2},{6,4},{8,6},{10,8},{12,10},{14,12},{16,14},{18,16},{20... | collective-permute-start | bytes 3145736 | tf_op jit(solution)/shard_map/ppermute | solution.py:15
  241.1 36.2 %copy-start.1 = (s32[512,16]{0,1:T(8,128)S(1)}, s32[512,16]{0,1:T(8,128)}, u32[]{:S(2)}) copy-start(s32[512,16]{0,1:T(8,128)} %param.10) | copy-start | bytes 98308
where the time goes:
time: 282 us; the launch traced here: 278 us
  matrix products  91.4 us (32%)
  waiting for transfers between devices  46.1 us (16%)
  local copies, waits for them, and re-layouts  42.5 us (15%)
  starting transfers between devices  42.5 us (15%)
  other arithmetic  28.3 us (10%)
  blocking collectives  25.3 us (9%)
    ppermute x8, starting transfers between devices, shifted(): return lax.ppermute(shard, axis, pairs)  38.5 us
    all_to_all x1, blocking collectives, on_device(): lax.all_to_all(jnp.stack([query_out, key_out, value_out]), 'head', split_...  25.3 us
    dot_general x5, matrix products, score_grads(): jnp.einsum('qhd,khd->hqk', dout_heads, value_heads, preferred_element_typ...  25.3 us
    all_to_all x1, waiting for transfers between devices, on_device(): lax.all_to_all(entering, 'head', split_axis=2, concat_axis=1, tiled=True)  24.4 us
    dot_general x5, matrix products, key_value_grads(): jnp.einsum('hqk,qhd->khd', probs.astype(jnp.bfloat16), dout_heads, prefer...  22.1 us
    ppermute x8, waiting for transfers between devices, shifted(): return lax.ppermute(shard, axis, pairs)  21.6 us
    dot_general x5, matrix products, on_device(): jnp.einsum('hqk,khd->qhd', probs.astype(jnp.bfloat16), split_heads(remote...  19.1 us
    reduce_sum x3, other arithmetic, on_device(): row_total = row_total * jnp.exp(row_top - new_top) + jnp.sum(kept, axis=-1)  14.4 us
  transfers between devices with their start and end apart: 9, of which 5 were waited for; matrix products, arithmetic and copies ran while one was open for 15% of the time, Pallas kernels for 0%

commit v1 on v0

--- a/solution.py
+++ b/solution.py
@@ -138,8 +138,15 @@
     query_out = (query_grad * score_scale).astype(jnp.bfloat16).reshape(frames, feature_cols)
     key_out = (collected[0] * score_scale).astype(jnp.bfloat16).reshape(frames, feature_cols)
     value_out = collected[1].astype(jnp.bfloat16).reshape(frames, feature_cols)
-    leaving = lax.all_to_all(
-        jnp.stack([query_out, key_out, value_out]), "head", split_axis=1, concat_axis=2, tiled=True
+    frame_in = jnp.stack([query_out, key_out, value_out])
+    leaving = jnp.concatenate(
+        lax.all_to_all(
+            jnp.stack(jnp.split(frame_in, lax.axis_size("head"), axis=1)),
+            "head",
+            split_axis=0,
+            concat_axis=0,
+        ),
+        2,
     )
     return (leaving[0], leaving[1], leaving[2])
 

time: 282 us -> 262 us (0.929)
  other arithmetic: 28.3 us -> 18.2 us
  blocking collectives: 25.3 us -> 15.4 us
  local copies, waits for them, and re-layouts: 42.5 us -> 34.3 us
  waiting for transfers between devices: 46.1 us -> 52.9 us
    all_to_all x1, blocking collectives: 25.3 us -> 15.4 us  [on_device(): lax.all_to_all(jnp.stack(jnp.split(frame_in, lax.axis_size('head'), axis=...]
    ppermute x8, waiting for transfers between devices: 21.6 us -> 28.4 us  [shifted(): return lax.ppermute(shard, axis, pairs)]
    slice x4 -> x1, local copies, waits for them, and re-layouts: 4.68 us -> 0.1 us  [on_device(): return (leaving[0], leaving[1], leaving[2])]
    another operation x5, other arithmetic: 4.4 us -> 0.49 us  [key_value_grads(): return jnp.stack([key_part, value_part]).astype(jnp.bfloat16)]
    convert_element_type x2 -> x0, local copies, waits for them, and re-layouts: 3.29 us -> none  [the longest x1 2.41 us: on_device(): (collected[0] * score_scale).astype(jnp.bfloat16)]
    another operation x1 -> x2, other arithmetic: 3.57 us -> 0.32 us  [the longest x1 0.17 us: on_device(): frame_in = jnp.stack([query_out, key_out, value_out])]
    squeeze x0 -> x3, local copies, waits for them, and re-layouts: none -> 3 us  [on_device(): return (leaving[0], leaving[1], leaving[2])]
where the time goes in v1:
time: 262 us; the launch traced here: 256 us
  matrix products  91.4 us (35%)
  waiting for transfers between devices  52.9 us (20%)
  starting transfers between devices  42.7 us (16%)
  local copies, waits for them, and re-layouts  34.3 us (13%)
  other arithmetic  18.2 us (7%)
  blocking collectives  15.4 us (6%)
    ppermute x8, starting transfers between devices, shifted(): return lax.ppermute(shard, axis, pairs)  38.7 us
    ppermute x8, waiting for transfers between devices, shifted(): return lax.ppermute(shard, axis, pairs)  28.4 us
    dot_general x5, matrix products, score_grads(): jnp.einsum('qhd,khd->hqk', dout_heads, value_heads, preferred_element_typ...  25.3 us
    all_to_all x1, waiting for transfers between devices, on_device(): lax.all_to_all(entering, 'head', split_axis=2, concat_axis=1, tiled=True)  24.4 us
    dot_general x5, matrix products, key_value_grads(): jnp.einsum('hqk,qhd->khd', probs.astype(jnp.bfloat16), dout_heads, prefer...  22.1 us
    dot_general x5, matrix products, on_device(): jnp.einsum('hqk,khd->qhd', probs.astype(jnp.bfloat16), split_heads(remote...  19.1 us
    all_to_all x1, blocking collectives, on_device(): lax.all_to_all(jnp.stack(jnp.split(frame_in, lax.axis_size('head'), axis=...  15.4 us
    reduce_sum x3, other arithmetic, on_device(): row_total = row_total * jnp.exp(row_top - new_top) + jnp.sum(kept, axis=-1)  14.3 us
  transfers between devices with their start and end apart: 9, of which 5 were waited for; matrix products, arithmetic and copies ran while one was open for 15% of the time, Pallas kernels for 0%

profile of v1, /device:TPU:121, one launch (start us, length us, event | category | flops | bytes accessed | tf_op | source)
XLA Modules:
  0.0 256.4 jit_solution(13974273214401376049)
XLA Ops:
  0.6 1.8 pad_maximum_fusion
  2.4 2.6 %copy.104 = bf16[4,256,1024]{1,0,2:T(4,128)(2,1)} copy(bf16[4,256,1024]{2,1,0:T(8,128)(2,1)S(1)} %pad_maximum_fusion) | data formatting | bytes 4194304 | tf_op jit(solution)/shard_map/stack | solution.py:59
  5.1 4.0 %all-to-all-start = ((bf16[4,256,1024]{1,0,2:T(4,128)(2,1)}), bf16[4,256,1024]{1,0,2:T(4,128)(2,1)S(1)}, u32[]{:S(2)}, u32[]{:S(2)}) async-start(bf16[4,256,1024]{1,0,2:T(4,128)(2,1)} %copy.104), calls=%async_computation | async-start | bytes 4194304 | tf_op jit(solution)/shard_map/all_to_all | solution.py:60
  10.0 24.4 %all-to-all-done = bf16[4,256,1024]{1,0,2:T(4,128)(2,1)S(1)} async-done(((bf16[4,256,1024]{1,0,2:T(4,128)(2,1)}), bf16[4,256,1024]{1,0,2:T(4,128)(2,1)S(1)}, u32[]{:S(2)}, u32[]{:S(2)}) %all-to-all-start) | async-done | bytes 2097184 | tf_op jit(solution)/shard_map/all_to_all | solution.py:60
  34.5 1.3 copy-done.5
  35.8 3.7 %copy.169 = bf16[4,256,2,512]{1,2,3,0:T(2,128)(2,1)S(1)} copy(bf16[4,256,2,512]{1,0,3,2:T(4,128)(2,1)} %bitcast.158) | data formatting | bytes 4194304 | tf_op jit(solution)/shard_map/all_to_all | solution.py:60
  40.3 1.5 slice.97
  41.8 3.8 %collective-permute-start.1 = (bf16[2,512,512]{1,2,0:T(8,128)(2,1)}, bf16[2,512,512]{1,2,0:T(8,128)(2,1)}, u32[]{:S(2)}, u32[]{:S(2)}) collective-permute-start(bf16[2,512,512]{1,2,0:T(8,128)(2,1)} %slice.97), channel_id=1, source_target_pairs={{2,0},{4,2},{6,4},{8,6},{10,8},{12,10},{14,12},{16,14},{18,16},{20... | collective-permute-start | bytes 3145736 | tf_op jit(solution)/shard_map/ppermute | solution.py:15
  45.7 6.2 %collective-permute-start = (bf16[2,512,512]{1,2,0:T(8,128)(2,1)}, bf16[2,512,512]{1,2,0:T(8,128)(2,1)}, u32[]{:S(2)}, u32[]{:S(2)}) collective-permute-start(bf16[2,512,512]{1,2,0:T(8,128)(2,1)} %slice.97), channel_id=1, source_target_pairs={{0,2},{2,4},{4,6},{6,8},{8,10},{10,12},{12,14},{14,16},{16,18},{18... | collective-permute-start | bytes 3145736 | tf_op jit(solution)/shard_map/ppermute | solution.py:15
  55.0 1.0 broadcast_in_dim.149
  56.0 1.8 broadcast_in_dim.150
  57.9 1.0 broadcast_in_dim.144
  58.9 1.8 broadcast_in_dim.145
  60.7 2.4 fusion.43
  63.1 1.4 reshape_squeeze.52
  64.4 1.4 reshape_squeeze.47
  65.8 1.4 reshape_squeeze.46
  67.2 2.2 reshape_squeeze.53
  69.4 1.5 fusion.5
  70.9 1.9 collective-permute-start.3
  72.8 1.3 fusion.46
  74.1 8.1 %collective-permute-start.2 = (bf16[2,512,512]{1,2,0:T(8,128)(2,1)}, bf16[2,512,512]{1,2,0:T(8,128)(2,1)S(1)}, u32[]{:S(2)}, u32[]{:S(2)}) collective-permute-start(bf16[2,512,512]{1,2,0:T(8,128)(2,1)} %collective-permute-done), channel_id=1, source_target_pairs={{0,2},{2,4},{4,6},{6,8},{8,10},{10,12},{12,14},{14,16},{16,18},{18... | collective-permute-start | bytes 3145736 | tf_op jit(solution)/shard_map/ppermute | solution.py:15
  82.2 1.3 fusion.47
  83.5 1.5 fusion.7
  85.0 1.5 fusion.6
  86.5 4.9 %collective-permute-done.3 = bf16[2,512,512]{1,2,0:T(8,128)(2,1)S(1)} collective-permute-done((bf16[2,512,512]{1,2,0:T(8,128)(2,1)}, bf16[2,512,512]{1,2,0:T(8,128)(2,1)S(1)}, u32[]{:S(2)}, u32[]{:S(2)}) %collective-permute-start.3) | collective-permute-done | bytes 1048608 | tf_op jit(solution)/shard_map/ppermute | solution.py:15
  91.5 4.7 %fusion.9 = (f32[8,512]{1,0:T(8,128)S(1)}, f32[8,512,512]{1,2,0:T(8,128)}) fusion(pred[512,512]{0,1:T(8,128)(4,1)S(1)} %broadcast_in_dim.159, bf16[512,8,64]{0,2,1:T(8,128)(2,1)S(1)} %reshape_squeeze.47, bf16[512,8,64]{0,2,1:T(8,128)(2,1)S(1)} %bitcast.166), kind=kOutput, calls=%fused_computation.29 | convolution fusion | flops 274722816 | bytes 9715712 | tf_op jit(solution)/shard_map/qhd,khd->hqk/dot_general | solution.py:35
  96.3 4.7 %fusion.8 = (f32[8,512]{1,0:T(8,128)S(1)}, f32[8,512,512]{1,2,0:T(8,128)}) fusion(pred[512,512]{0,1:T(8,128)(4,1)S(1)} %broadcast_in_dim.156, bf16[512,8,64]{0,2,1:T(8,128)(2,1)S(1)} %reshape_squeeze.47, bf16[512,8,64]{0,2,1:T(8,128)(2,1)S(1)} %bitcast.160), kind=kOutput, calls=%fused_computation.28 | convolution fusion | flops 274722816 | bytes 9715712 | tf_op jit(solution)/shard_map/qhd,khd->hqk/dot_general | solution.py:35
  101.0 2.4 select_reduce_fusion.4
  103.5 7.9 %select_reduce_fusion = (f32[8,512]{1,0:T(8,128)S(1)}, f32[8,512]{1,0:T(8,128)S(1)}) fusion(f32[8,512,512]{1,2,0:T(8,128)} %get-tuple-element.31, f32[8,512]{1,0:T(8,128)S(1)} %get-tuple-element.3, pred[512,512]{0,1:T(8,128)(4,1)S(1)} %broadcast_in_dim.159, f32[8,512]{1,0:T(8,128)S(1)} %get-tuple-element.4, f32[8,512,512]{1,2,0:T(8,128)} %get-tuple-element.33, ...), kind=kLoop, calls=%fused_computation.10 | loop fusion | flops 20963328 | bytes 17367040 | tf_op jit(solution)/shard_map/reduce_sum | solution.py:106
  111.4 4.0 %select_reduce_fusion.2 = (f32[8,512]{1,0:T(8,128)S(1)}, f32[8,512]{1,0:T(8,128)S(1)}) fusion(f32[8,512,512]{1,2,0:T(8,128)S(1)} %get-tuple-element.35, f32[8,512]{1,0:T(8,128)S(1)} %get-tuple-element.5, pred[512,512]{0,1:T(8,128)(4,1)S(1)} %broadcast_in_dim.153, f32[8,512]{1,0:T(8,128)S(1)} %get-tuple-element.6, f32[8,512,512]{1,2,0:T(8,128)S(1)} %get-tuple-element.37, ...), kind=kLoop, calls=%fused_computation.12 | loop fusion | flops 20963328 | bytes 17367040 | tf_op jit(solution)/shard_map/reduce_sum | solution.py:106
  115.4 6.5 %fusion.26 = bf16[1,512,8,64]{1,3,2,0:T(8,128)(2,1)} fusion(bf16[512,8,64]{0,2,1:T(8,128)(2,1)S(1)} %reshape_squeeze.52, f32[8,512,512]{1,2,0:T(8,128)} %get-tuple-element.31, f32[8,512]{1,0:T(8,128)S(1)} %log_add_fusion, pred[512,512]{0,1:T(8,128)(4,1)S(1)} %broadcast_in_dim.159), kind=kOutput, calls=%fused_computation.67 | convolution fusion | flops 279183360 | bytes 9715712 | tf_op jit(solution)/shard_map/hqk,qhd->khd/dot_general | solution.py:48
  121.9 6.5 %fusion.24 = bf16[1,512,8,64]{1,3,2,0:T(8,128)(2,1)} fusion(bf16[512,8,64]{0,2,1:T(8,128)(2,1)S(1)} %reshape_squeeze.52, f32[8,512,512]{1,2,0:T(8,128)} %get-tuple-element.33, f32[8,512]{1,0:T(8,128)S(1)} %log_add_fusion, pred[512,512]{0,1:T(8,128)(4,1)S(1)} %broadcast_in_dim.156), kind=kOutput, calls=%fused_computation.65 | convolution fusion | flops 279183360 | bytes 9715712 | tf_op jit(solution)/shard_map/hqk,qhd->khd/dot_general | solution.py:48
  128.4 5.8 %fusion.36 = f32[8,64,512]{2,1,0:T(8,128)S(1)} fusion(bf16[512,8,64]{0,2,1:T(8,128)(2,1)S(1)} %bitcast.178, f32[8,512,512]{1,2,0:T(8,128)} %get-tuple-element.31, f32[8,512]{1,0:T(8,128)S(1)} %log_add_fusion, pred[512,512]{0,1:T(8,128)(4,1)S(1)} %broadcast_in_dim.159), kind=kOutput, calls=%fused_computation.85 | convolution fusion | flops 278921216 | bytes 10240000 | tf_op jit(solution)/shard_map/hqk,khd->qhd/dot_general | solution.py:116
  134.2 2.6 fusion.39
  136.8 2.4 convolution_add_fusion.5
  139.2 2.4 convolution_add_fusion.4
  141.7 5.9 %fusion.16 = f32[512,8]{0,1:T(8,128)S(1)} fusion(f32[8,64,512]{2,1,0:T(8,128)S(1)} %fusion.36, f32[8,64,512]{2,1,0:T(8,128)S(1)} %convolution_add_fusion.4, bf16[512,8,64]{0,2,1:T(8,128)(2,1)S(1)} %bitcast.180, bf16[512,8,64]{0,2,1:T(8,128)(2,1)S(1)} %reshape_squeeze.52, f32[8,512,512]{1,2,0:T(8,128)} %get-tuple-element.33, f32[8,512]{1,0:T(8,128)S(1)} %log_add_fusion, ...), kind=kOutput, calls=%fused_computation.57 | convolution fusion | flops 280227840 | bytes 11829248 | tf_op jit(solution)/shard_map/hqk,khd->qhd/dot_general | solution.py:116
  147.6 6.9 %multiply_convert_fusion = bf16[8,512,512]{1,2,0:T(8,128)(2,1)} fusion(f32[8,512,512]{1,2,0:T(8,128)} %get-tuple-element.31, f32[8,512]{1,0:T(8,128)S(1)} %bitcast.186, f32[8,512]{1,0:T(8,128)S(1)} %log_add_fusion, pred[512,512]{0,1:T(8,128)(4,1)S(1)} %broadcast_in_dim.159, bf16[512,8,64]{0,2,1:T(8,128)(2,1)S(1)} %reshape_squeeze.52, ...), kind=kOutput, calls=%fused_computation | convolution fusion | flops 283115520 | bytes 13926400 | tf_op jit(solution)/shard_map/qhd,khd->hqk/dot_general | solution.py:40
  154.4 6.8 %multiply_convert_fusion.1 = bf16[8,512,512]{1,2,0:T(8,128)(2,1)} fusion(f32[8,512,512]{1,2,0:T(8,128)} %get-tuple-element.33, f32[8,512]{1,0:T(8,128)S(1)} %bitcast.187, f32[8,512]{1,0:T(8,128)S(1)} %log_add_fusion, pred[512,512]{0,1:T(8,128)(4,1)S(1)} %broadcast_in_dim.156, bf16[512,8,64]{0,2,1:T(8,128)(2,1)S(1)} %reshape_squeeze.52, ...), kind=kOutput, calls=%fused_computation.1 | convolution fusion | flops 283115520 | bytes 13926400 | tf_op jit(solution)/shard_map/qhd,khd->hqk/dot_general | solution.py:40
  161.3 3.3 %fusion.22 = bf16[1,512,8,64]{1,3,2,0:T(8,128)(2,1)} fusion(bf16[512,8,64]{0,2,1:T(8,128)(2,1)S(1)} %reshape_squeeze.52, f32[8,512,512]{1,2,0:T(8,128)S(1)} %get-tuple-element.35, f32[8,512]{1,0:T(8,128)S(1)} %log_add_fusion, pred[512,512]{0,1:T(8,128)(4,1)S(1)} %broadcast_in_dim.153), kind=kOutput, calls=%fused_computation.63 | convolution fusion | flops 279183360 | bytes 9715712 | tf_op jit(solution)/shard_map/hqk,qhd->khd/dot_general | solution.py:48
  164.6 4.8 %multiply_convert_fusion.2 = bf16[8,512,512]{1,2,0:T(8,128)(2,1)} fusion(f32[8,512,512]{1,2,0:T(8,128)S(1)} %get-tuple-element.35, f32[8,512]{1,0:T(8,128)S(1)} %bitcast.188, f32[8,512]{1,0:T(8,128)S(1)} %log_add_fusion, pred[512,512]{0,1:T(8,128)(4,1)S(1)} %broadcast_in_dim.153, bf16[512,8,64]{0,2,1:T(8,128)(2,1)S(1)} %reshape_squeeze.52, ...), kind=kOutput, calls=%fused_computation.2 | convolution fusion | flops 283115520 | bytes 13926400 | tf_op jit(solution)/shard_map/qhd,khd->hqk/dot_general | solution.py:40
  169.4 3.3 %fusion.20 = bf16[1,512,8,64]{1,3,2,0:T(8,128)(2,1)} fusion(bf16[512,8,64]{0,2,1:T(8,128)(2,1)S(1)} %reshape_squeeze.52, f32[8,512,512]{1,2,0:T(8,128)S(1)} %get-tuple-element.37, f32[8,512]{1,0:T(8,128)S(1)} %log_add_fusion, pred[512,512]{0,1:T(8,128)(4,1)S(1)} %broadcast_in_dim.150), kind=kOutput, calls=%fused_computation.61 | convolution fusion | flops 279183360 | bytes 9715712 | tf_op jit(solution)/shard_map/hqk,qhd->khd/dot_general | solution.py:48
  172.6 3.4 %multiply_convert_fusion.3 = bf16[8,512,512]{1,2,0:T(8,128)(2,1)S(1)} fusion(f32[8,512,512]{1,2,0:T(8,128)S(1)} %get-tuple-element.37, f32[8,512]{1,0:T(8,128)S(1)} %bitcast.189, f32[8,512]{1,0:T(8,128)S(1)} %log_add_fusion, pred[512,512]{0,1:T(8,128)(4,1)S(1)} %broadcast_in_dim.150, bf16[512,8,64]{0,2,1:T(8,128)(2,1)S(1)} %reshape_squeeze.52, ...), kind=kOutput, calls=%fused_computation.3 | convolution fusion | flops 283115520 | bytes 13926400 | tf_op jit(solution)/shard_map/qhd,khd->hqk/dot_general | solution.py:40
  176.1 2.5 fusion.18
  178.6 3.4 %multiply_convert_fusion.4 = bf16[8,512,512]{1,2,0:T(8,128)(2,1)S(1)} fusion(f32[8,512,512]{1,2,0:T(8,128)S(1)} %get-tuple-element.39, f32[8,512]{1,0:T(8,128)S(1)} %bitcast.190, f32[8,512]{1,0:T(8,128)S(1)} %log_add_fusion, pred[512,512]{0,1:T(8,128)(4,1)S(1)} %broadcast_in_dim.145, bf16[512,8,64]{0,2,1:T(8,128)(2,1)S(1)} %reshape_squeeze.52, ...), kind=kOutput, calls=%fused_computation.4 | convolution fusion | flops 283115520 | bytes 13926400 | tf_op jit(solution)/shard_map/qhd,khd->hqk/dot_general | solution.py:40
  182.1 1.4 fusion.17
  184.3 1.4 fusion.25
  185.8 2.1 collective-permute-start.7
  187.9 1.4 fusion.23
  189.4 3.7 %collective-permute-start.6 = (bf16[2,512,8,64]{1,3,2,0:T(8,128)(2,1)S(1)}, bf16[2,512,8,64]{1,3,2,0:T(8,128)(2,1)S(1)}, u32[]{:S(2)}, u32[]{:S(2)}) collective-permute-start(bf16[2,512,8,64]{1,3,2,0:T(8,128)(2,1)S(1)} %pad_maximum_fusion.6), channel_id=1, source_target_pairs={{4,0},{6,2},{8,4},{10,6},{12,8},{14,10},{16,12},{18,14},{20,16},{2... | collective-permute-start | bytes 3145736 | tf_op jit(solution)/shard_map/ppermute | solution.py:15
  193.2 1.4 fusion.21
  194.7 11.1 %collective-permute-start.5 = (bf16[2,512,8,64]{1,3,2,0:T(8,128)(2,1)S(1)}, bf16[2,512,8,64]{1,3,2,0:T(8,128)(2,1)S(1)}, u32[]{:S(2)}, u32[]{:S(2)}) collective-permute-start(bf16[2,512,8,64]{1,3,2,0:T(8,128)(2,1)S(1)} %pad_maximum_fusion.5), channel_id=1, source_target_pairs={{0,2},{2,4},{4,6},{6,8},{8,10},{10,12},{12,14},{14,16},{16,18},{18... | collective-permute-start | bytes 3145736 | tf_op jit(solution)/shard_map/ppermute | solution.py:15
  205.7 1.4 fusion.19
  207.2 1.9 collective-permute-start.4
  210.1 0.8 fusion.51
  212.5 3.0 %collective-permute-done.6 = bf16[2,512,8,64]{1,3,2,0:T(8,128)(2,1)S(1)} collective-permute-done((bf16[2,512,8,64]{1,3,2,0:T(8,128)(2,1)S(1)}, bf16[2,512,8,64]{1,3,2,0:T(8,128)(2,1)S(1)}, u32[]{:S(2)}, u32[]{:S(2)}) %collective-permute-start.6) | collective-permute-done | bytes 1048608 | tf_op jit(solution)/shard_map/ppermute | solution.py:15
  215.6 6.5 %collective-permute-done.5 = bf16[2,512,8,64]{1,3,2,0:T(8,128)(2,1)S(1)} collective-permute-done((bf16[2,512,8,64]{1,3,2,0:T(8,128)(2,1)S(1)}, bf16[2,512,8,64]{1,3,2,0:T(8,128)(2,1)S(1)}, u32[]{:S(2)}, u32[]{:S(2)}) %collective-permute-start.5) | collective-permute-done | bytes 1048608 | tf_op jit(solution)/shard_map/ppermute | solution.py:15
  222.1 13.9 %collective-permute-done.4 = bf16[2,512,8,64]{1,3,2,0:T(8,128)(2,1)S(1)} collective-permute-done((bf16[2,512,8,64]{1,3,2,0:T(8,128)(2,1)S(1)}, bf16[2,512,8,64]{1,3,2,0:T(8,128)(2,1)S(1)}, u32[]{:S(2)}, u32[]{:S(2)}) %collective-permute-start.4) | collective-permute-done | bytes 1048608 | tf_op jit(solution)/shard_map/ppermute | solution.py:15
  236.0 0.9 convert_add_fusion
  237.6 15.4 %all_to_all.20 = bf16[2,3,256,512]{2,3,1,0:T(8,128)(2,1)S(1)} all-to-all(bf16[2,3,256,512]{2,3,1,0:T(8,128)(2,1)S(1)} %pad_maximum_fusion.2), channel_id=1, replica_groups=mesh['ctx'=64,'head'=2] {'head'}, dimensions={0} | all-to-all | bytes 3145728 | tf_op jit(solution)/shard_map/all_to_all | solution.py:143
  253.1 1.0 copy.165
  254.1 1.0 copy.166
  255.1 1.0 copy.167
  (77 shorter events, 9.7 us)
Async XLA Ops:
  0.6 8.4 %copy-start = (s32[512,16]{0,1:T(8,128)S(1)}, s32[512,16]{0,1:T(8,128)}, u32[]{:S(2)}) copy-start(s32[512,16]{0,1:T(8,128)} %param.10) | copy-start | bytes 98308
  5.1 29.4 %all-to-all-start = ((bf16[4,256,1024]{1,0,2:T(4,128)(2,1)}), bf16[4,256,1024]{1,0,2:T(4,128)(2,1)S(1)}, u32[]{:S(2)}, u32[]{:S(2)}) async-start(bf16[4,256,1024]{1,0,2:T(4,128)(2,1)} %copy.104), calls=%async_computation | async-start | bytes 4194304 | tf_op jit(solution)/shard_map/all_to_all | solution.py:60
  34.5 1.3 copy-start.5
  41.8 29.1 %collective-permute-start.1 = (bf16[2,512,512]{1,2,0:T(8,128)(2,1)}, bf16[2,512,512]{1,2,0:T(8,128)(2,1)}, u32[]{:S(2)}, u32[]{:S(2)}) collective-permute-start(bf16[2,512,512]{1,2,0:T(8,128)(2,1)} %slice.97), channel_id=1, source_target_pairs={{2,0},{4,2},{6,4},{8,6},{10,8},{12,10},{14,12},{16,14},{18,16},{20... | collective-permute-start | bytes 3145736 | tf_op jit(solution)/shard_map/ppermute | solution.py:15
  45.7 28.4 %collective-permute-start = (bf16[2,512,512]{1,2,0:T(8,128)(2,1)}, bf16[2,512,512]{1,2,0:T(8,128)(2,1)}, u32[]{:S(2)}, u32[]{:S(2)}) collective-permute-start(bf16[2,512,512]{1,2,0:T(8,128)(2,1)} %slice.97), channel_id=1, source_target_pairs={{0,2},{2,4},{4,6},{6,8},{8,10},{10,12},{12,14},{14,16},{16,18},{18... | collective-permute-start | bytes 3145736 | tf_op jit(solution)/shard_map/ppermute | solution.py:15
  70.9 20.5 %collective-permute-start.3 = (bf16[2,512,512]{1,2,0:T(8,128)(2,1)}, bf16[2,512,512]{1,2,0:T(8,128)(2,1)S(1)}, u32[]{:S(2)}, u32[]{:S(2)}) collective-permute-start(bf16[2,512,512]{1,2,0:T(8,128)(2,1)} %collective-permute-done.1), channel_id=1, source_target_pairs={{2,0},{4,2},{6,4},{8,6},{10,8},{12,10},{14,12},{16,14},{18,16},{20... | collective-permute-start | bytes 3145736 | tf_op jit(solution)/shard_map/ppermute | solution.py:15
  74.1 65.2 %copy-start.8 = (bf16[1,512,512]{1,2,0:T(8,128)(2,1)}, bf16[1,512,512]{1,2,0:T(8,128)(2,1)S(1)}, u32[]{:S(2)}) copy-start(bf16[1,512,512]{1,2,0:T(8,128)(2,1)S(1)} %get-tuple-element.18) | copy-start | bytes 1572868
  74.1 22.1 %collective-permute-start.2 = (bf16[2,512,512]{1,2,0:T(8,128)(2,1)}, bf16[2,512,512]{1,2,0:T(8,128)(2,1)S(1)}, u32[]{:S(2)}, u32[]{:S(2)}) collective-permute-start(bf16[2,512,512]{1,2,0:T(8,128)(2,1)} %collective-permute-done), channel_id=1, source_target_pairs={{0,2},{2,4},{4,6},{6,8},{8,10},{10,12},{12,14},{14,16},{16,18},{18... | collective-permute-start | bytes 3145736 | tf_op jit(solution)/shard_map/ppermute | solution.py:15
  83.4 53.3 %copy-start.10 = (bf16[1,512,512]{1,2,0:T(8,128)(2,1)}, bf16[1,512,512]{1,2,0:T(8,128)(2,1)S(1)}, u32[]{:S(2)}) copy-start(bf16[1,512,512]{1,2,0:T(8,128)(2,1)S(1)} %get-tuple-element.20) | copy-start | bytes 1572868
  91.5 36.9 %copy-start.12 = (bf16[1,512,512]{1,2,0:T(8,128)(2,1)}, bf16[1,512,512]{1,2,0:T(8,128)(2,1)S(1)}, u32[]{:S(2)}) copy-start(bf16[1,512,512]{1,2,0:T(8,128)(2,1)S(1)} %get-tuple-element.22) | copy-start | bytes 1572868
  96.3 45.4 %copy-start.13 = (bf16[1,512,512]{1,2,0:T(8,128)(2,1)}, bf16[1,512,512]{1,2,0:T(8,128)(2,1)S(1)}, u32[]{:S(2)}) copy-start(bf16[1,512,512]{1,2,0:T(8,128)(2,1)S(1)} %get-tuple-element.16) | copy-start | bytes 1572868
  128.4 5.8 %copy-start.6 = (bf16[512,8,64]{0,2,1:T(8,128)(2,1)S(1)}, bf16[512,8,64]{0,2,1:T(8,128)(2,1)}, u32[]{:S(2)}) copy-start(bf16[512,8,64]{0,2,1:T(8,128)(2,1)} %reshape_squeeze.53) | copy-start | bytes 1572868
  161.3 3.3 %copy-start.9 = (bf16[1,512,512]{1,2,0:T(8,128)(2,1)S(1)}, bf16[1,512,512]{1,2,0:T(8,128)(2,1)}, u32[]{:S(2)}) copy-start(bf16[1,512,512]{1,2,0:T(8,128)(2,1)} %copy-done.8) | copy-start | bytes 1572868
  169.3 3.3 %copy-start.11 = (bf16[1,512,512]{1,2,0:T(8,128)(2,1)S(1)}, bf16[1,512,512]{1,2,0:T(8,128)(2,1)}, u32[]{:S(2)}) copy-start(bf16[1,512,512]{1,2,0:T(8,128)(2,1)} %copy-done.10) | copy-start | bytes 1572868
  176.1 2.5 copy-start.7
  182.0 2.3 copy-start.3
  182.0 3.7 %copy-start.15 = (bf16[1,512,8,64]{1,3,2,0:T(8,128)(2,1)S(1)}, bf16[1,512,8,64]{1,3,2,0:T(8,128)(2,1)}, u32[]{:S(2)}) copy-start(bf16[1,512,8,64]{1,3,2,0:T(8,128)(2,1)} %fusion.26) | copy-start | bytes 1572868
  182.0 5.8 %copy-start.2 = (bf16[8,512,512]{1,2,0:T(8,128)(2,1)S(1)}, bf16[8,512,512]{1,2,0:T(8,128)(2,1)}, u32[]{:S(2)}) copy-start(bf16[8,512,512]{1,2,0:T(8,128)(2,1)} %multiply_convert_fusion.1) | copy-start | bytes 12582916
  183.4 5.8 %copy-start.14 = (bf16[1,512,8,64]{1,3,2,0:T(8,128)(2,1)S(1)}, bf16[1,512,8,64]{1,3,2,0:T(8,128)(2,1)}, u32[]{:S(2)}) copy-start(bf16[1,512,8,64]{1,3,2,0:T(8,128)(2,1)} %fusion.24) | copy-start | bytes 1572868
  184.3 8.9 %copy-start.4 = (bf16[8,512,512]{1,2,0:T(8,128)(2,1)S(1)}, bf16[8,512,512]{1,2,0:T(8,128)(2,1)}, u32[]{:S(2)}) copy-start(bf16[8,512,512]{1,2,0:T(8,128)(2,1)} %multiply_convert_fusion.2) | copy-start | bytes 12582916
  185.7 8.8 %copy-start.17 = (bf16[1,512,8,64]{1,3,2,0:T(8,128)(2,1)S(1)}, bf16[1,512,8,64]{1,3,2,0:T(8,128)(2,1)}, u32[]{:S(2)}) copy-start(bf16[1,512,8,64]{1,3,2,0:T(8,128)(2,1)} %fusion.22) | copy-start | bytes 1572868
  185.8 26.7 %collective-permute-start.7 = (bf16[2,512,8,64]{1,3,2,0:T(8,128)(2,1)S(1)}, bf16[2,512,8,64]{1,3,2,0:T(8,128)(2,1)S(1)}, u32[]{:S(2)}, u32[]{:S(2)}) collective-permute-start(bf16[2,512,8,64]{1,3,2,0:T(8,128)(2,1)S(1)} %pad_maximum_fusion.7), channel_id=1, source_target_pairs={{0,4},{2,6},{4,8},{6,10},{8,12},{10,14},{12,16},{14,18},{16,20},{1... | collective-permute-start | bytes 3145736 | tf_op jit(solution)/shard_map/ppermute | solution.py:15
  189.3 17.8 %copy-start.16 = (bf16[1,512,8,64]{1,3,2,0:T(8,128)(2,1)S(1)}, bf16[1,512,8,64]{1,3,2,0:T(8,128)(2,1)}, u32[]{:S(2)}) copy-start(bf16[1,512,8,64]{1,3,2,0:T(8,128)(2,1)} %fusion.20) | copy-start | bytes 1572868
  189.4 26.1 %collective-permute-start.6 = (bf16[2,512,8,64]{1,3,2,0:T(8,128)(2,1)S(1)}, bf16[2,512,8,64]{1,3,2,0:T(8,128)(2,1)S(1)}, u32[]{:S(2)}, u32[]{:S(2)}) collective-permute-start(bf16[2,512,8,64]{1,3,2,0:T(8,128)(2,1)S(1)} %pad_maximum_fusion.6), channel_id=1, source_target_pairs={{4,0},{6,2},{8,4},{10,6},{12,8},{14,10},{16,12},{18,14},{20,16},{2... | collective-permute-start | bytes 3145736 | tf_op jit(solution)/shard_map/ppermute | solution.py:15
  194.7 27.4 %collective-permute-start.5 = (bf16[2,512,8,64]{1,3,2,0:T(8,128)(2,1)S(1)}, bf16[2,512,8,64]{1,3,2,0:T(8,128)(2,1)S(1)}, u32[]{:S(2)}, u32[]{:S(2)}) collective-permute-start(bf16[2,512,8,64]{1,3,2,0:T(8,128)(2,1)S(1)} %pad_maximum_fusion.5), channel_id=1, source_target_pairs={{0,2},{2,4},{4,6},{6,8},{8,10},{10,12},{12,14},{14,16},{16,18},{18... | collective-permute-start | bytes 3145736 | tf_op jit(solution)/shard_map/ppermute | solution.py:15
  207.2 28.8 %collective-permute-start.4 = (bf16[2,512,8,64]{1,3,2,0:T(8,128)(2,1)S(1)}, bf16[2,512,8,64]{1,3,2,0:T(8,128)(2,1)S(1)}, u32[]{:S(2)}, u32[]{:S(2)}) collective-permute-start(bf16[2,512,8,64]{1,3,2,0:T(8,128)(2,1)S(1)} %pad_maximum_fusion.4), channel_id=1, source_target_pairs={{2,0},{4,2},{6,4},{8,6},{10,8},{12,10},{14,12},{16,14},{18,16},{20... | collective-permute-start | bytes 3145736 | tf_op jit(solution)/shard_map/ppermute | solution.py:15
  237.1 19.0 %copy-start.1 = (s32[512,16]{0,1:T(8,128)S(1)}, s32[512,16]{0,1:T(8,128)}, u32[]{:S(2)}) copy-start(s32[512,16]{0,1:T(8,128)} %param.10) | copy-start | bytes 98308
